TPU v7x, 512 devices: a whole 4x8x8 slice. The times are simulated.
512 devices in a mesh: leaf: 8 (over z), row: 8 (over y), col: 8 (over x, core).
Axes of the slice: x: 4, y: 8, z: 8, core: 2. Of those that a mesh axis runs over, the one named last changes fastest.
Arguments:
- child_inverse: bfloat16 [8, 2, 3072, 3072], P('leaf', None, 'row', 'col'), as said below
- child_rhs: bfloat16 [8, 2, 3072, 256], P('leaf', None, 'col'), may hold values from -6 to 6
- child_to_mid: bfloat16 [8, 2, 2048, 3072], P('leaf', None, ('row', 'col')), may hold values from -0.109375 to 0.109375
- child_to_root: bfloat16 [8, 2, 2048, 3072], P('leaf', None, ('row', 'col')), may hold values from -0.109375 to 0.109375
- mid_rows_list: int32 [8, 2, 2048], P('leaf'), may hold values from 0 to 4095, as said below
- root_rows_list: int32 [8, 2, 2048], P('leaf'), may hold values from 0 to 8191, as said below
- mid_inverse: bfloat16 [8, 4096, 4096], P('leaf', 'row', 'col'), as said below
- mid_rhs: bfloat16 [8, 4096, 256], P('leaf', 'col'), may hold values from -6 to 6
- mid_to_root: bfloat16 [8, 2048, 4096], P('leaf', ('row', 'col')), may hold values from -0.09375 to 0.09375
- mid_root_list: int32 [8, 2048], P('leaf'), may hold values from 0 to 8191, as said below
- root_inverse: bfloat16 [8192, 8192], P(('leaf', 'row'), 'col'), as said below
- root_rhs: bfloat16 [8192, 256], P('col'), may hold values from -6 to 6
Outputs:
- child_solution: bfloat16 [8, 2, 3072, 256], P('leaf', None, 'row')
- mid_solution: bfloat16 [8, 4096, 256], P('leaf', 'row')
- root_solution: bfloat16 [8192, 256], P(('leaf', 'row'))
Inputs may be any that keep to these rules, and one draw needn't show every extreme that they name: `mid_rows_list`: each list of a child holds 2048 distinct rows of its middle supernode in increasing order, always with the first and the last. `root_rows_list`: each list of a child holds 2048 distinct rows of the root in increasing order, always with the first and the last. `mid_root_list`: each list holds 2048 distinct rows of the root in increasing order, always with the first and the last. `child_inverse`: lower triangular with a positive diagonal. `mid_inverse`: lower triangular with a positive diagonal. `root_inverse`: lower triangular with a positive diagonal.
All inputs are finite; a program needn't handle non-finite values.
Results may differ from a plain program's by a relative error of at most 0.0085.
Values may be sent and summed in bfloat16 or wider, within the bound.
A program may use at most 64 MiB of HBM per device.

v0:
```python
import jax
import jax.numpy as jnp
from jax import lax
from jax.sharding import PartitionSpec as P


def solve_spread(partial_value):
    placed = lax.psum(partial_value, "col").astype(jnp.bfloat16)
    whole_rows = lax.all_gather(placed, "row", axis=2, tiled=True)
    return (placed, whole_rows)


def gather_updates(pieces):
    return lax.all_gather(pieces, ("row", "col"), axis=2, tiled=True)


def scatter_block(values, rows_list, piece_rows, col_index):
    width = values.shape[-1]
    flat_values = values.reshape(-1, width).astype(jnp.float32)
    offsets = rows_list.reshape(-1) - col_index * piece_rows
    inside = (offsets >= 0) & (offsets < piece_rows)
    target = jnp.where(inside, offsets, piece_rows)
    summed = jnp.zeros((piece_rows + 1, width), jnp.float32).at[target].add(flat_values)
    return summed[:piece_rows]


def per_device(
    child_inverse,
    child_rhs,
    child_to_mid,
    child_to_root,
    mid_rows_list,
    root_rows_list,
    mid_inverse,
    mid_rhs,
    mid_to_root,
    mid_root_list,
    root_inverse,
    root_rhs,
):
    grid_size = lax.axis_size("row") * lax.axis_size("col")
    col_index = lax.axis_index("col")
    rhs_width = child_rhs.shape[3]
    child_partial = jnp.einsum(
        "gcij,gcjr->gcir", child_inverse, child_rhs, preferred_element_type=jnp.float32
    )
    child_local, child_whole = solve_spread(child_partial)
    mid_piece = child_to_mid.shape[2]
    root_piece = child_to_root.shape[2]
    update_mid = jnp.einsum(
        "gcuj,gcjr->gcur", child_to_mid, child_whole, preferred_element_type=jnp.float32
    ).astype(jnp.bfloat16)
    update_root = jnp.einsum(
        "gcuj,gcjr->gcur", child_to_root, child_whole, preferred_element_type=jnp.float32
    ).astype(jnp.bfloat16)
    stacked = jnp.concatenate((update_mid, update_root), axis=2)
    gathered = gather_updates(stacked)
    lead_count = gathered.shape[0]
    child_count = gathered.shape[1]
    split_view = gathered.reshape(
        lead_count, child_count, grid_size, mid_piece + root_piece, rhs_width
    )
    mid_updates = split_view[:, :, :, :mid_piece].reshape(
        lead_count, child_count, grid_size * mid_piece, rhs_width
    )
    root_updates = split_view[:, :, :, mid_piece:].reshape(
        lead_count, child_count, grid_size * root_piece, rhs_width
    )
    root_group = root_rhs.shape[0]
    child_root_term = scatter_block(root_updates, root_rows_list, root_group, col_index)
    mid_term = scatter_block(mid_updates, mid_rows_list, mid_rhs.shape[1], col_index)
    mid_input = (mid_rhs[0].astype(jnp.float32) - mid_term).astype(jnp.bfloat16)
    mid_partial = jnp.dot(mid_inverse[0], mid_input, preferred_element_type=jnp.float32)[None, None]
    mid_local, mid_whole = solve_spread(mid_partial)
    update_top = jnp.dot(
        mid_to_root[0], mid_whole[0, 0], preferred_element_type=jnp.float32
    ).astype(jnp.bfloat16)[None, None]
    top_whole = gather_updates(update_top)
    top_term = scatter_block(top_whole, mid_root_list, root_group, col_index)
    root_sum = lax.psum(child_root_term + top_term, "leaf")
    root_input = (root_rhs.astype(jnp.float32) - root_sum).astype(jnp.bfloat16)
    root_partial = jnp.dot(root_inverse, root_input, preferred_element_type=jnp.float32)
    root_solution = lax.psum(root_partial, "col").astype(jnp.bfloat16)
    return (child_local, mid_local[0], root_solution)


def solution(mesh):
    in_specs = (
        P("leaf", None, "row", "col"),
        P("leaf", None, "col", None),
        P("leaf", None, ("row", "col"), None),
        P("leaf", None, ("row", "col"), None),
        P("leaf", None, None),
        P("leaf", None, None),
        P("leaf", "row", "col"),
        P("leaf", "col", None),
        P("leaf", ("row", "col"), None),
        P("leaf", None),
        P(("leaf", "row"), "col"),
        P("col", None),
    )
    out_specs = (P("leaf", None, "row", None), P("leaf", "row", None), P(("leaf", "row"), None))
    return jax.shard_map(
        per_device, mesh=mesh, in_specs=in_specs, out_specs=out_specs, check_vma=False
    )
```

profile of v0, /device:TPU:8, one launch (start us, length us, event | category | flops | bytes accessed | tf_op | source)
XLA Modules:
  0.0 500.9 jit_solution(5121878186767649496)
XLA Ops:
  7.2 0.0 all-gather.6.cloned.1.call-start
  7.2 1.0 copy-done
  8.2 1.4 convolution_bitcast_fusion
  9.6 32.4 %all-reduce.6 = bf16[1,2,384,256]{3,2,1,0:T(8,128)(2,1)} all-reduce(f32[1,2,384,256]{3,2,1,0:T(8,128)S(1)} %convolution_bitcast_fusion), channel_id=1, replica_groups=mesh['leaf'=8,'row'=8,'col'=8] {'col'}, use_global_device_ids=true, to_apply=%region_0.0 | all-reduce | flops 196608 | bytes 1179648 | tf_op jit(solution)/shard_map/psum | solution.py:8
  42.0 0.0 all-gather.6.cloned.1.call-update
  42.0 0.0 all-gather.8.cloned.1.call-start
  42.1 49.2 %all-gather.6.cloned.1.call-done = bf16[1,2,3072,256]{3,2,1,0:T(8,128)(2,1)} async-done(((bf16[1,2,384,256]{3,2,1,0:T(8,128)(2,1)}), bf16[1,2,3072,256]{3,2,1,0:T(8,128)(2,1)}) %all-gather.6.cloned.1.call-update) | async-done | bytes 3145744 | tf_op jit(solution)/shard_map/all_gather | solution.py:9
  91.3 2.7 fusion.18
  94.0 0.1 copy-done.1
  94.1 0.6 fusion.21
  94.8 0.6 pad_maximum_fusion
  95.5 0.0 all-gather.10.cloned.1.call-start
  95.6 82.8 %all-gather.8.cloned.1.call-done = bf16[1,2,4096,256]{3,2,1,0:T(8,128)(2,1)} async-done(((bf16[1,2,64,256]{3,2,1,0:T(8,128)(2,1)}), bf16[1,2,4096,256]{3,2,1,0:T(8,128)(2,1)}) %all-gather.8.cloned.1.call-update) | async-done | bytes 4194320 | tf_op jit(solution)/shard_map/all_gather | solution.py:14
  178.4 4.2 fusion.42
  182.6 28.5 %scatter_custom_fusion = f32[513,256]{1,0:T(8,128)S(1)} fusion(s32[4096]{0:T(1024)S(1)} %bitcast.88, bf16[4096,256]{1,0:T(8,128)(2,1)} %bitcast.83, f32[]{:T(128)} %constant.7.clone.1), kind=kCustom, calls=%fused_computation.5 | custom fusion | flops 2097152 | bytes 2622468 | tf_op jit(solution)/shard_map/scatter-add | solution.py:23
  211.2 2.2 convolution_bitcast_fusion.1
  213.4 32.1 %all-reduce.7 = bf16[1,1,512,256]{2,3,1,0:T(8,128)(2,1)} all-reduce(f32[1,1,512,256]{2,3,1,0:T(8,128)} %convolution_bitcast_fusion.1), channel_id=1, replica_groups=mesh['leaf'=8,'row'=8,'col'=8] {'col'}, use_global_device_ids=true, to_apply=%region_2.3 | all-reduce | flops 131072 | bytes 786432 | tf_op jit(solution)/shard_map/psum | solution.py:8
  245.4 0.0 all-gather.10.cloned.1.call-update
  245.5 0.0 all-gather.12.cloned.1.call-start
  245.5 40.1 %all-gather.10.cloned.1.call-done = bf16[1,1,4096,256]{2,3,1,0:T(8,128)(2,1)} async-done(((bf16[1,1,512,256]{2,3,1,0:T(8,128)(2,1)}), bf16[1,1,4096,256]{2,3,1,0:T(8,128)(2,1)}) %all-gather.10.cloned.1.call-update) | async-done | bytes 2097168 | tf_op jit(solution)/shard_map/all_gather | solution.py:9
  285.7 2.9 fusion.27
  288.6 0.0 all-gather.12.cloned.1.call-update
  288.6 0.0 all-reduce.5.cloned.1.call-start
  288.8 29.2 %scatter_custom_fusion.1 = f32[1025,256]{1,0:T(8,128)} fusion(s32[4096]{0:T(1024)S(1)} %bitcast.89, bf16[4096,256]{1,0:T(8,128)(2,1)S(1)} %bitcast.82, f32[]{:T(128)} %constant.7.clone.1), kind=kCustom, calls=%fused_computation.3 | custom fusion | flops 2097152 | bytes 3146756 | tf_op jit(solution)/shard_map/scatter-add | solution.py:23
  318.0 51.5 %all-gather.12.cloned.1.call-done = bf16[2048,256]{1,0:T(8,128)(2,1)} async-done(((bf16[32,256]{1,0:T(8,128)(2,1)}), bf16[2048,256]{1,0:T(8,128)(2,1)}) %all-gather.12.cloned.1.call-update) | async-done | bytes 1048592 | tf_op jit(solution)/shard_map/all_gather | solution.py:14
  369.5 14.9 %scatter_custom_fusion.2 = f32[1025,256]{1,0:T(8,128)S(1)} fusion(s32[2048]{0:T(1024)S(1)} %bitcast.90, bf16[2048,256]{1,0:T(8,128)(2,1)} %all-gather.12.cloned.1.call-done, f32[]{:T(128)} %constant.7.clone.1), kind=kCustom, calls=%fused_computation.13 | custom fusion | flops 1048576 | bytes 2098180 | tf_op jit(solution)/shard_map/scatter-add | solution.py:23
  384.4 1.2 slice_add_fusion
  385.6 0.8 copy.17
  386.5 80.8 %all-reduce.5.cloned.1.call-done = f32[1024,256]{1,0:T(8,128)} async-done(((f32[1024,256]{1,0:T(8,128)}), f32[1024,256]{1,0:T(8,128)}) %all-reduce.5.cloned.1.call-update) | async-done | bytes 1048592 | tf_op jit(solution)/shard_map/psum | solution.py:80
  467.3 1.6 convolution_bitcast_fusion.2
  468.9 24.7 %all-reduce.8 = bf16[128,256]{0,1:T(8,128)(2,1)S(1)} all-reduce(f32[128,256]{0,1:T(8,128)S(1)} %convolution_bitcast_fusion.2), channel_id=1, replica_groups=mesh['leaf'=8,'row'=8,'col'=8] {'col'}, use_global_device_ids=true, to_apply=%region_6.7 | all-reduce | flops 32768 | bytes 196608 | tf_op jit(solution)/shard_map/psum | solution.py:83
  493.6 0.7 copy.18
  (29 shorter events, 0.2 us)
Async XLA Ops:
  7.2 1.1 copy-start
  7.2 84.1 %copy-start.5 = (bf16[1,2,32,3072]{3,2,1,0:T(8,128)(2,1)S(1)}, bf16[1,2,32,3072]{3,2,1,0:T(8,128)(2,1)}, u32[]{:S(2)}) copy-start(bf16[1,2,32,3072]{3,2,1,0:T(8,128)(2,1)} %param.14) | copy-start | bytes 1179652
  7.2 84.1 %all-gather.6.cloned.1.call-start = ((), (), s32[]{:S(2)}) async-start(), calls=%async_computation | async-start | bytes 3538944 | tf_op jit(solution)/shard_map/all_gather | solution.py:9
  42.0 52.0 %copy-start.6 = (bf16[1,2,32,3072]{3,2,1,0:T(8,128)(2,1)S(1)}, bf16[1,2,32,3072]{3,2,1,0:T(8,128)(2,1)}, u32[]{:S(2)}) copy-start(bf16[1,2,32,3072]{3,2,1,0:T(8,128)(2,1)} %param.15) | copy-start | bytes 1179652
  42.0 136.4 %all-gather.8.cloned.1.call-start = ((), (), s32[]{:S(2)}) async-start(), calls=%async_computation.1 | async-start | bytes 4259840 | tf_op jit(solution)/shard_map/all_gather | solution.py:14
  91.3 2.8 copy-start.1
  94.1 1.4 copy-start.8
  95.5 190.2 %all-gather.10.cloned.1.call-start = ((), (), s32[]{:S(2)}) async-start(), calls=%async_computation.2 | async-start | bytes 2359296 | tf_op jit(solution)/shard_map/all_gather | solution.py:9
  182.6 28.5 %copy-start.7 = (bf16[1,512,256]{2,1,0:T(8,128)(2,1)S(1)}, bf16[1,512,256]{2,1,0:T(8,128)(2,1)}, u32[]{:S(2)}) copy-start(bf16[1,512,256]{2,1,0:T(8,128)(2,1)} %param.19) | copy-start | bytes 786436
  213.4 75.3 %copy-start.9 = (s32[1,2,2048]{2,1,0:T(2,128)S(1)}, s32[1,2,2048]{2,1,0:T(2,128)}, u32[]{:S(2)}) copy-start(s32[1,2,2048]{2,1,0:T(2,128)} %param.17) | copy-start | bytes 49156
  213.4 75.4 %copy-start.10 = (s32[1,2048]{1,0:T(1,128)S(1)}, s32[1,2048]{1,0:T(1,128)}, u32[]{:S(2)}) copy-start(s32[1,2048]{1,0:T(1,128)} %param.21) | copy-start | bytes 24580
  245.5 124.1 %all-gather.12.cloned.1.call-start = ((), (), s32[]{:S(2)}) async-start(), calls=%async_computation.4 | async-start | bytes 1064960 | tf_op jit(solution)/shard_map/all_gather | solution.py:14
  288.6 178.7 %all-reduce.5.cloned.1.call-start = ((), (), s32[]{:S(2)}) async-start(), calls=%async_computation.3 | async-start | bytes 2097152 | tf_op jit(solution)/shard_map/psum | solution.py:80
  318.0 66.4 %copy-start.2 = (f32[1025,256]{1,0:T(8,128)S(1)}, f32[1025,256]{1,0:T(8,128)}, u32[]{:S(2)}) copy-start(f32[1025,256]{1,0:T(8,128)} %scatter_custom_fusion.1) | copy-start | bytes 3148804
  384.4 1.2 copy-start.3
  384.4 82.9 %copy-start.4 = (bf16[1024,256]{1,0:T(8,128)(2,1)S(1)}, bf16[1024,256]{1,0:T(8,128)(2,1)}, u32[]{:S(2)}) copy-start(bf16[1024,256]{1,0:T(8,128)(2,1)} %param.23) | copy-start | bytes 1572868
Sparse Core Ops, SparseCore 0:
  42.2 49.0 all-gather.5
  95.6 82.8 all-gather.7
  245.6 40.0 all-gather.9
  289.4 80.0 all-gather.11
  385.8 81.4 all-reduce.4
where the time goes:
time: 501 us
  waiting for transfers between devices  305 us (61%)
  blocking collectives  89.2 us (18%)
  other arithmetic  74.5 us (15%)
  between operations  14 us (3%)
  matrix products  11.4 us (2%)
  local copies, waits for them, and re-layouts  7.04 us (1%)
    all_gather x2, waiting for transfers between devices, gather_updates(): return lax.all_gather(pieces, ('row', 'col'), axis=2, tiled=True)  134 us
    all_gather x2, waiting for transfers between devices, solve_spread(): whole_rows = lax.all_gather(placed, 'row', axis=2, tiled=True)  89.3 us
    psum x1, waiting for transfers between devices, per_device(): root_sum = lax.psum(child_root_term + top_term, 'leaf')  80.8 us
    scatter-add x3, other arithmetic, scatter_block(): jnp.zeros((piece_rows + 1, width), jnp.float32).at[target].add(flat_values)  72.6 us
    psum x2, blocking collectives, solve_spread(): placed = lax.psum(partial_value, 'col').astype(jnp.bfloat16)  64.5 us
    psum x1, blocking collectives, per_device(): root_solution = lax.psum(root_partial, 'col').astype(jnp.bfloat16)  24.7 us
  transfers between devices with their start and end apart: 5, of which 5 were waited for; matrix products, arithmetic and copies ran while one was open for 6% of the time, Pallas kernels for 0%

commit v1 on v0

--- a/solution.py
+++ b/solution.py
@@ -2,6 +2,13 @@
 import jax.numpy as jnp
 from jax import lax
 from jax.sharding import PartitionSpec as P
+
+
+def exchange_gather(x, name, dim):
+    n_dev = lax.axis_size(name)
+    blocks = jnp.stack([x for _ in range(n_dev)])
+    blocks = lax.all_to_all(blocks, name, split_axis=0, concat_axis=0)
+    return jnp.concatenate(blocks, axis=dim)
 
 
 def solve_spread(partial_value):
@@ -11,7 +18,7 @@
 
 
 def gather_updates(pieces):
-    return lax.all_gather(pieces, ("row", "col"), axis=2, tiled=True)
+    return exchange_gather(pieces, ("row", "col"), 2)
 
 
 def scatter_block(values, rows_list, piece_rows, col_index):

time: 501 us -> 482 us (0.962)
  waiting for transfers between devices: 305 us -> 266 us
  starting transfers between devices: 0.2 us -> 16.9 us
    all_gather x2 -> x0, waiting for transfers between devices: 134 us -> none  [gather_updates(): return lax.all_gather(pieces, ('row', 'col'), axis=2, tiled=True)]
    all_to_all x0 -> x2, waiting for transfers between devices: none -> 95.1 us  [exchange_gather(): blocks = lax.all_to_all(blocks, name, split_axis=0, concat_axis=0)]
    all_to_all x0 -> x2, starting transfers between devices: none -> 16.8 us  [exchange_gather(): blocks = lax.all_to_all(blocks, name, split_axis=0, concat_axis=0)]
  transfers between devices with their start and end apart: 5 -> 5, of which waited for: 5 -> 4; matrix products, arithmetic and copies ran while one was open for 6% -> 6% of each run, Pallas kernels for 0% -> 0%
where the time goes in v1:
time: 482 us
  waiting for transfers between devices  266 us (55%)
  blocking collectives  89.5 us (19%)
  other arithmetic  73.9 us (15%)
  starting transfers between devices  16.9 us (4%)
  between operations  14 us (3%)
  matrix products  10.8 us (2%)
  local copies, waits for them, and re-layouts  10.7 us (2%)
    all_to_all x2, waiting for transfers between devices, exchange_gather(): blocks = lax.all_to_all(blocks, name, split_axis=0, concat_axis=0)  95.1 us
    all_gather x2, waiting for transfers between devices, solve_spread(): whole_rows = lax.all_gather(placed, 'row', axis=2, tiled=True)  87.6 us
    psum x1, waiting for transfers between devices, per_device(): root_sum = lax.psum(child_root_term + top_term, 'leaf')  83.2 us
    scatter-add x3, other arithmetic, scatter_block(): jnp.zeros((piece_rows + 1, width), jnp.float32).at[target].add(flat_values)  72.6 us
    psum x2, blocking collectives, solve_spread(): placed = lax.psum(partial_value, 'col').astype(jnp.bfloat16)  64.8 us
    psum x1, blocking collectives, per_device(): root_solution = lax.psum(root_partial, 'col').astype(jnp.bfloat16)  24.7 us
    all_to_all x2, starting transfers between devices, exchange_gather(): blocks = lax.all_to_all(blocks, name, split_axis=0, concat_axis=0)  16.8 us
  transfers between devices with their start and end apart: 5, of which 4 were waited for; matrix products, arithmetic and copies ran while one was open for 6% of the time, Pallas kernels for 0%

profile of v1, /device:TPU:8, one launch (start us, length us, event | category | flops | bytes accessed | tf_op | source)
XLA Modules:
  0.0 481.8 jit_solution(18130020414846556612)
XLA Ops:
  7.2 0.0 all-gather.3.cloned.1.call-start
  7.2 1.0 copy-done
  8.2 1.4 convolution_bitcast_fusion
  9.6 32.4 %all-reduce.6 = bf16[1,2,384,256]{3,2,1,0:T(8,128)(2,1)} all-reduce(f32[1,2,384,256]{3,2,1,0:T(8,128)S(1)} %convolution_bitcast_fusion), channel_id=1, replica_groups=mesh['leaf'=8,'row'=8,'col'=8] {'col'}, use_global_device_ids=true, to_apply=%region_0.0 | all-reduce | flops 196608 | bytes 1179648 | tf_op jit(solution)/shard_map/psum | solution.py:15
  42.0 0.0 all-gather.3.cloned.1.call-update
  42.0 49.3 %all-gather.3.cloned.1.call-done = bf16[1,2,3072,256]{3,2,1,0:T(8,128)(2,1)} async-done(((bf16[1,2,384,256]{3,2,1,0:T(8,128)(2,1)}), bf16[1,2,3072,256]{3,2,1,0:T(8,128)(2,1)}) %all-gather.3.cloned.1.call-update) | async-done | bytes 3145744 | tf_op jit(solution)/shard_map/all_gather | solution.py:16
  91.3 2.7 fusion.18
  94.0 0.1 copy-done.1
  94.1 0.6 fusion.21
  94.8 2.5 stack.4
  97.3 8.7 %all-to-all-start = ((bf16[64,1,2,64,256]{4,3,2,1,0:T(8,128)(2,1)}), bf16[64,1,2,64,256]{4,3,2,1,0:T(8,128)(2,1)}, u32[]{:S(2)}, u32[]{:S(2)}) async-start(bf16[64,1,2,64,256]{4,3,2,1,0:T(8,128)(2,1)} %stack.4), calls=%async_computation | async-start | bytes 8388608 | tf_op jit(solution)/shard_map/all_to_all | solution.py:10
  106.0 0.0 all-gather.5.cloned.1.call-start
  106.1 95.1 %all-to-all-done = bf16[64,1,2,64,256]{4,3,2,1,0:T(8,128)(2,1)} async-done(((bf16[64,1,2,64,256]{4,3,2,1,0:T(8,128)(2,1)}), bf16[64,1,2,64,256]{4,3,2,1,0:T(8,128)(2,1)}, u32[]{:S(2)}, u32[]{:S(2)}) %all-to-all-start) | async-done | bytes 4194336 | tf_op jit(solution)/shard_map/all_to_all | solution.py:10
  201.2 2.5 copy.27
  203.7 1.8 fusion.42
  205.5 28.5 %scatter_custom_fusion = f32[513,256]{1,0:T(8,128)S(1)} fusion(s32[4096]{0:T(1024)S(1)} %bitcast.94, bf16[4096,256]{1,0:T(8,128)(2,1)} %bitcast.90, f32[]{:T(128)} %constant.7.clone.1), kind=kCustom, calls=%fused_computation.5 | custom fusion | flops 2097152 | bytes 2622468 | tf_op jit(solution)/shard_map/scatter-add | solution.py:30
  234.0 2.2 convolution_bitcast_fusion.1
  236.2 32.4 %all-reduce.7 = bf16[1,1,512,256]{2,3,1,0:T(8,128)(2,1)} all-reduce(f32[1,1,512,256]{2,3,1,0:T(8,128)} %convolution_bitcast_fusion.1), channel_id=1, replica_groups=mesh['leaf'=8,'row'=8,'col'=8] {'col'}, use_global_device_ids=true, to_apply=%region_2.3 | all-reduce | flops 131072 | bytes 786432 | tf_op jit(solution)/shard_map/psum | solution.py:15
  268.6 0.0 all-gather.5.cloned.1.call-update
  268.6 38.3 %all-gather.5.cloned.1.call-done = bf16[1,1,4096,256]{2,3,1,0:T(8,128)(2,1)} async-done(((bf16[1,1,512,256]{2,3,1,0:T(8,128)(2,1)}), bf16[1,1,4096,256]{2,3,1,0:T(8,128)(2,1)}) %all-gather.5.cloned.1.call-update) | async-done | bytes 2097168 | tf_op jit(solution)/shard_map/all_gather | solution.py:16
  306.9 2.3 fusion.27
  309.3 1.1 stack.5
  310.4 8.1 %all-to-all-start.1 = ((bf16[64,1,1,32,256]{4,3,2,1,0:T(8,128)(2,1)}), bf16[64,1,1,32,256]{4,3,2,1,0:T(8,128)(2,1)}, u32[]{:S(2)}, u32[]{:S(2)}) async-start(bf16[64,1,1,32,256]{4,3,2,1,0:T(8,128)(2,1)} %stack.5), calls=%async_computation.1 | async-start | bytes 2097152 | tf_op jit(solution)/shard_map/all_to_all | solution.py:10
  318.5 0.0 all-reduce.5.cloned.1.call-start
  318.7 29.2 %scatter_custom_fusion.1 = f32[1025,256]{1,0:T(8,128)} fusion(s32[4096]{0:T(1024)S(1)} %bitcast.95, bf16[4096,256]{1,0:T(8,128)(2,1)S(1)} %bitcast.89, f32[]{:T(128)} %constant.7.clone.1), kind=kCustom, calls=%fused_computation.3 | custom fusion | flops 2097152 | bytes 3146756 | tf_op jit(solution)/shard_map/scatter-add | solution.py:30
  348.0 14.9 %scatter_custom_fusion.2 = f32[1025,256]{1,0:T(8,128)S(1)} fusion(s32[2048]{0:T(1024)S(1)} %bitcast.96, bf16[2048,256]{1,0:T(8,128)(2,1)} %bitcast.34, f32[]{:T(128)} %constant.7.clone.1), kind=kCustom, calls=%fused_computation.12 | custom fusion | flops 1048576 | bytes 2098180 | tf_op jit(solution)/shard_map/scatter-add | solution.py:30
  362.9 1.1 slice_add_fusion
  364.1 0.8 copy.22
  364.9 83.2 %all-reduce.5.cloned.1.call-done = f32[1024,256]{1,0:T(8,128)} async-done(((f32[1024,256]{1,0:T(8,128)}), f32[1024,256]{1,0:T(8,128)}) %all-reduce.5.cloned.1.call-update) | async-done | bytes 1048592 | tf_op jit(solution)/shard_map/psum | solution.py:87
  448.1 1.6 convolution_bitcast_fusion.2
  449.8 24.7 %all-reduce.8 = bf16[128,256]{0,1:T(8,128)(2,1)S(1)} all-reduce(f32[128,256]{0,1:T(8,128)S(1)} %convolution_bitcast_fusion.2), channel_id=1, replica_groups=mesh['leaf'=8,'row'=8,'col'=8] {'col'}, use_global_device_ids=true, to_apply=%region_6.7 | all-reduce | flops 32768 | bytes 196608 | tf_op jit(solution)/shard_map/psum | solution.py:90
  474.5 0.7 copy.23
  (30 shorter events, 0.2 us)
Async XLA Ops:
  7.2 1.1 copy-start
  7.2 84.1 %copy-start.5 = (bf16[1,2,32,3072]{3,2,1,0:T(8,128)(2,1)S(1)}, bf16[1,2,32,3072]{3,2,1,0:T(8,128)(2,1)}, u32[]{:S(2)}) copy-start(bf16[1,2,32,3072]{3,2,1,0:T(8,128)(2,1)} %param.14) | copy-start | bytes 1179652
  7.2 84.1 %all-gather.3.cloned.1.call-start = ((), (), s32[]{:S(2)}) async-start(), calls=%async_computation.2 | async-start | bytes 3538944 | tf_op jit(solution)/shard_map/all_gather | solution.py:16
  42.0 52.0 %copy-start.6 = (bf16[1,2,32,3072]{3,2,1,0:T(8,128)(2,1)S(1)}, bf16[1,2,32,3072]{3,2,1,0:T(8,128)(2,1)}, u32[]{:S(2)}) copy-start(bf16[1,2,32,3072]{3,2,1,0:T(8,128)(2,1)} %param.15) | copy-start | bytes 1179652
  91.3 2.8 copy-start.1
  97.3 8.8 %copy-start.8 = (s32[1,2,2048]{2,1,0:T(2,128)S(1)}, s32[1,2,2048]{2,1,0:T(2,128)}, u32[]{:S(2)}) copy-start(s32[1,2,2048]{2,1,0:T(2,128)} %param.16) | copy-start | bytes 49156
  97.3 103.9 %all-to-all-start = ((bf16[64,1,2,64,256]{4,3,2,1,0:T(8,128)(2,1)}), bf16[64,1,2,64,256]{4,3,2,1,0:T(8,128)(2,1)}, u32[]{:S(2)}, u32[]{:S(2)}) async-start(bf16[64,1,2,64,256]{4,3,2,1,0:T(8,128)(2,1)} %stack.4), calls=%async_computation | async-start | bytes 8388608 | tf_op jit(solution)/shard_map/all_to_all | solution.py:10
  106.0 201.0 %all-gather.5.cloned.1.call-start = ((), (), s32[]{:S(2)}) async-start(), calls=%async_computation.3 | async-start | bytes 2359296 | tf_op jit(solution)/shard_map/all_gather | solution.py:16
  205.5 28.5 %copy-start.7 = (bf16[1,512,256]{2,1,0:T(8,128)(2,1)S(1)}, bf16[1,512,256]{2,1,0:T(8,128)(2,1)}, u32[]{:S(2)}) copy-start(bf16[1,512,256]{2,1,0:T(8,128)(2,1)} %param.19) | copy-start | bytes 786436
  309.3 9.3 %copy-start.9 = (s32[1,2,2048]{2,1,0:T(2,128)S(1)}, s32[1,2,2048]{2,1,0:T(2,128)}, u32[]{:S(2)}) copy-start(s32[1,2,2048]{2,1,0:T(2,128)} %param.17) | copy-start | bytes 49156
  309.3 9.4 %copy-start.10 = (s32[1,2048]{1,0:T(1,128)S(1)}, s32[1,2048]{1,0:T(1,128)}, u32[]{:S(2)}) copy-start(s32[1,2048]{1,0:T(1,128)} %param.21) | copy-start | bytes 24580
  310.4 37.5 %all-to-all-start.1 = ((bf16[64,1,1,32,256]{4,3,2,1,0:T(8,128)(2,1)}), bf16[64,1,1,32,256]{4,3,2,1,0:T(8,128)(2,1)}, u32[]{:S(2)}, u32[]{:S(2)}) async-start(bf16[64,1,1,32,256]{4,3,2,1,0:T(8,128)(2,1)} %stack.5), calls=%async_computation.1 | async-start | bytes 2097152 | tf_op jit(solution)/shard_map/all_to_all | solution.py:10
  318.5 129.6 %all-reduce.5.cloned.1.call-start = ((), (), s32[]{:S(2)}) async-start(), calls=%async_computation.4 | async-start | bytes 2097152 | tf_op jit(solution)/shard_map/psum | solution.py:87
  347.9 14.9 %copy-start.2 = (f32[1025,256]{1,0:T(8,128)S(1)}, f32[1025,256]{1,0:T(8,128)}, u32[]{:S(2)}) copy-start(f32[1025,256]{1,0:T(8,128)} %scatter_custom_fusion.1) | copy-start | bytes 3148804
  362.9 1.2 copy-start.3
  362.9 85.2 %copy-start.4 = (bf16[1024,256]{1,0:T(8,128)(2,1)S(1)}, bf16[1024,256]{1,0:T(8,128)(2,1)}, u32[]{:S(2)}) copy-start(bf16[1024,256]{1,0:T(8,128)(2,1)} %param.23) | copy-start | bytes 1572868
Sparse Core Ops, SparseCore 0:
  42.2 49.0 all-gather.2
  268.7 38.1 all-gather.4
  364.2 83.8 all-reduce.4
